TPU v7x, 128 devices: a whole 4x4x4 slice. The times are simulated.
128 devices in a mesh: grid: 32 (over y_lo, x, z), ch: 4 (over y_hi, core).
Axes of the slice: x: 4, y: 4 (y_hi: 2, y_lo: 2; y = y_hi * 2 + y_lo), z: 4, core: 2. Of those that a mesh axis runs over, the one named last changes fastest.
Arguments:
- inputs: bfloat16 [128, 1024, 512], P('grid', None, 'ch'), may hold values from -6 to 6
- w_gate: bfloat16 [512, 512], P(None, 'ch'), may hold values from -0.25 to 0.25
- w_value: bfloat16 [512, 512], P(None, 'ch'), may hold values from -0.25 to 0.25
- short_filter: bfloat16 [2, 3, 3, 512], P(None, None, None, 'ch'), may hold values from -2 to 2
- row_filter: bfloat16 [1024, 512], P(None, 'ch'), may hold values from -0.1875 to 0.1875
- column_filter: bfloat16 [128, 512], P(None, 'ch'), may hold values from -0.5 to 0.5
- cotangent: bfloat16 [128, 1024, 512], P('grid', None, 'ch'), may hold values from -6 to 6
Outputs:
- gated: bfloat16 [128, 1024, 512], P('grid', None, 'ch')
- input_grad: bfloat16 [128, 1024, 512], P('grid', None, 'ch')
- gate_grad: float32 [512, 512], P('grid', 'ch')
- value_grad: float32 [512, 512], P('grid', 'ch')
- short_grad: float32 [2, 3, 3, 512], P(None, None, None, 'ch')
- row_grad: float32 [1024, 512], P('grid', 'ch')
- column_grad: float32 [128, 512], P('grid', 'ch')
All inputs are finite; a program needn't handle non-finite values.
Results may differ from a plain program's by a relative error of at most 0.025.
Values may be sent and summed in bfloat16 or wider, within the bound.
No kernel may reach another device: no remote copies, remote signals or barrier semaphores. Data moves between devices by JAX's collectives and lax.ppermute only.
A program may use at most 128 MiB of HBM per device.

v0:
```python
import math
import jax
import jax.numpy as jnp
from jax import lax
from jax.sharding import PartitionSpec as P

highest = lax.Precision.HIGHEST


def extended(value, sides, width):
    for axis, dim in sides:
        size, length = (lax.axis_size(axis), value.shape[dim])
        up = [(i, (i + 1) % size) for i in range(size - 1)]
        down = [(j, i) for i, j in up]
        last = lax.slice_in_dim(value, length - width, length, axis=dim)
        initial = lax.slice_in_dim(value, 0, width, axis=dim)
        before = lax.ppermute(last, axis, up)
        after = lax.ppermute(initial, axis, down)
        value = jnp.concatenate([before, value, after], axis=dim)
    return value


def sent_to_all(value, axis):
    copies = jnp.broadcast_to(value, (lax.axis_size(axis), *value.shape))
    return lax.all_to_all(copies, axis, split_axis=0, concat_axis=0, tiled=True)


def taken_together(value, axis):
    return sent_to_all(value, axis).sum(axis=0)


def in_one_piece(arrays, axis, dim, along):
    both = jnp.concatenate(arrays, axis=along)
    out, at, finished = (lax.psum_scatter(both, axis, scatter_dimension=dim, tiled=True), 0, [])
    for a in arrays:
        finished.append(lax.slice_in_dim(out, at, at + a.shape[along], axis=along))
        at += a.shape[along]
    return tuple(finished)


def hartley(length):
    position = jnp.arange(length, dtype=jnp.int32)
    product = position[:, None] * position[None, :] % length
    phases = product.astype(jnp.float32) * (2.0 * math.pi / length)
    return jnp.cos(phases) + jnp.sin(phases)


def mirror(values, along):
    leading = lax.slice_in_dim(values, 0, 1, axis=along)
    remainder = lax.slice_in_dim(values, 1, values.shape[along], axis=along)
    return jnp.concatenate([leading, jnp.flip(remainder, along)], axis=along)


def even_odd(spectrum, along):
    reversed_spec = mirror(spectrum, along)
    return (0.5 * (spectrum + reversed_spec), 0.5 * (spectrum - reversed_spec))


def column_forward(row_cols, cas_height, col_even, col_odd):
    spec_rows = jnp.einsum("hwc,hk->kwc", row_cols, cas_height, precision=highest)
    second = spec_rows * col_even[:, None] + mirror(spec_rows, 0) * col_odd[:, None]
    mixed_cols = (
        jnp.einsum("kwc,kh->hwc", second, cas_height, precision=highest) / cas_height.shape[0]
    )
    return (spec_rows, mixed_cols)


def column_backward(grad_cols, spec_rows, cas_height, col_even, col_odd, scale):
    full_height = cas_height.shape[0]
    spec_grad = jnp.einsum("hwc,hk->kwc", grad_cols, cas_height, precision=highest)
    mirrored_grad = mirror(spec_grad, 0)
    back_cols = spec_grad * col_even[:, None] - mirrored_grad * col_odd[:, None]
    grad_row_cols = (
        jnp.einsum("kwc,kh->hwc", back_cols, cas_height, precision=highest) / full_height
    )
    rows_even, rows_odd = even_odd(spec_rows, 0)
    col_term = jnp.sum(spec_grad * rows_even - mirrored_grad * rows_odd, axis=1)
    col_grad = jnp.einsum("kc,km->mc", col_term, cas_height, precision=highest) * (
        scale / full_height
    )
    return (grad_row_cols, col_grad)


def local(inputs, w_gate, w_value, short_filter, row_filter, column_filter, cotangent):
    tile_rows, full_width, channels = inputs.shape
    gathered = lax.all_gather(inputs, "ch", axis=2, tiled=True)
    w_both = jnp.concatenate([w_gate, w_value], axis=1)
    stacked = jnp.einsum(
        "rwd,dc->rwc", gathered, w_both, preferred_element_type=jnp.float32
    ).astype(jnp.bfloat16)
    kernel = jnp.concatenate([short_filter[0], short_filter[1]], axis=-1).astype(jnp.float32)
    framed = extended(stacked, (("grid", 0),), 1)
    framed = jnp.pad(framed, ((0, 0), (1, 1), (0, 0))).astype(jnp.float32)
    featured = jnp.zeros((tile_rows, full_width, 2 * channels), jnp.float32)
    for row_shift in range(3):
        for col_shift in range(3):
            featured = (
                featured
                + kernel[row_shift, col_shift]
                * framed[row_shift : row_shift + tile_rows, col_shift : col_shift + full_width]
            )
    featured = featured.astype(jnp.bfloat16)
    gate_feat = featured[..., :channels].astype(jnp.float32)
    value_bf = featured[..., channels:]
    cas_width = hartley(full_width)
    width_high = cas_width.astype(jnp.bfloat16)
    width_low = (cas_width - width_high.astype(jnp.float32)).astype(jnp.bfloat16)
    spec_b = jnp.einsum("rwc,wk->rkc", value_bf, width_high, preferred_element_type=jnp.float32)
    spec_b = spec_b + jnp.einsum(
        "rwc,wk->rkc", value_bf, width_low, preferred_element_type=jnp.float32
    )
    row_spec = jnp.einsum("mc,mk->kc", row_filter.astype(jnp.float32), cas_width, precision=highest)
    row_even, row_odd = even_odd(row_spec, 0)
    row_mixed = spec_b * row_even + mirror(spec_b, 1) * row_odd
    mix_row = jnp.einsum("rkc,kw->rwc", row_mixed, cas_width, precision=highest) / full_width
    full_height = column_filter.shape[0]
    cas_height = hartley(full_height)
    col_spec = jnp.einsum(
        "mc,mk->kc", column_filter.astype(jnp.float32), cas_height, precision=highest
    )
    col_even, col_odd = even_odd(col_spec, 0)
    scale = 1.0 / math.sqrt(full_height * full_width)
    grad_out = cotangent.astype(jnp.float32)
    grad_mix = grad_out * gate_feat
    row_cols = lax.all_to_all(mix_row, "grid", split_axis=1, concat_axis=0, tiled=True)
    spec_rows, mixed_cols = column_forward(row_cols, cas_height, col_even, col_odd)
    mix_col = lax.all_to_all(mixed_cols, "grid", split_axis=0, concat_axis=1, tiled=True)
    grad_cols = lax.all_to_all(grad_mix, "grid", split_axis=1, concat_axis=0, tiled=True)
    grad_row_cols, col_grad = column_backward(
        grad_cols, spec_rows, cas_height, col_even, col_odd, scale
    )
    grad_row = lax.all_to_all(grad_row_cols, "grid", split_axis=0, concat_axis=1, tiled=True)
    gated = (gate_feat * mix_col).astype(jnp.bfloat16)
    grad_gate = grad_out * mix_col
    spec_gr = jnp.einsum("rwc,wk->rkc", grad_row, cas_width, precision=highest)
    mirrored_gr = mirror(spec_gr, 1)
    back_rows = spec_gr * row_even - mirrored_gr * row_odd
    grad_value = jnp.einsum("rkc,kw->rwc", back_rows, cas_width, precision=highest) / full_width
    value_even, value_odd = even_odd(spec_b, 1)
    row_term = jnp.sum(spec_gr * value_even - mirrored_gr * value_odd, axis=0)
    row_grad = jnp.einsum("kc,km->mc", row_term, cas_width, precision=highest) * (
        scale / full_width
    )
    grad_feat = jnp.concatenate([grad_gate, grad_value], axis=2)
    grad_framed = extended(grad_feat, (("grid", 0),), 1)
    grad_framed = jnp.pad(grad_framed, ((0, 0), (1, 1), (0, 0)))
    back_sum = jnp.zeros((tile_rows, full_width, 2 * channels), jnp.float32)
    short_rows = []
    for row_shift in range(3):
        short_cols = []
        for col_shift in range(3):
            back_sum = (
                back_sum
                + kernel[row_shift, col_shift]
                * grad_framed[
                    2 - row_shift : 2 - row_shift + tile_rows,
                    2 - col_shift : 2 - col_shift + full_width,
                ]
            )
            short_cols.append(
                jnp.sum(
                    grad_feat
                    * framed[row_shift : row_shift + tile_rows, col_shift : col_shift + full_width],
                    axis=(0, 1),
                )
            )
        short_rows.append(jnp.stack(short_cols))
    back_stack = back_sum.astype(jnp.bfloat16)
    short_term = jnp.stack(short_rows).reshape(3, 3, 2, channels).transpose(2, 0, 1, 3) * scale
    short_grad = taken_together(short_term, "grid")
    weight_term = (
        jnp.einsum("rwd,rwc->dc", gathered, back_stack, preferred_element_type=jnp.float32) * scale
    )
    gate_grad, value_grad, row_share, col_share = (
        *tuple(
            (
                part.astype(jnp.float32)
                for part in in_one_piece(
                    (
                        weight_term[:, :channels].astype(jnp.bfloat16),
                        weight_term[:, channels:].astype(jnp.bfloat16),
                    ),
                    "grid",
                    0,
                    1,
                )
            )
        ),
        lax.psum_scatter(
            row_grad.astype(jnp.bfloat16), "grid", scatter_dimension=0, tiled=True
        ).astype(jnp.float32),
        lax.psum_scatter(
            col_grad.astype(jnp.bfloat16), "grid", scatter_dimension=0, tiled=True
        ).astype(jnp.float32),
    )
    partial_term = jnp.einsum("rwc,dc->rwd", back_stack, w_both, preferred_element_type=jnp.float32)
    input_grad = lax.psum_scatter(
        partial_term.astype(jnp.bfloat16), "ch", scatter_dimension=2, tiled=True
    )
    return (gated, input_grad, gate_grad, value_grad, short_grad, row_share, col_share)


def solution(mesh):
    return jax.shard_map(
        local,
        mesh=mesh,
        in_specs=(
            P("grid", None, "ch"),
            P(None, "ch"),
            P(None, "ch"),
            P(None, None, None, "ch"),
            P(None, "ch"),
            P(None, "ch"),
            P("grid", None, "ch"),
        ),
        out_specs=(
            P("grid", None, "ch"),
            P("grid", None, "ch"),
            P("grid", "ch"),
            P("grid", "ch"),
            P(None, None, None, "ch"),
            P("grid", "ch"),
            P("grid", "ch"),
        ),
        check_vma=False,
    )
```

profile of v0, /device:TPU:1, one launch (start us, length us, event | category | flops | bytes accessed | tf_op | source)
XLA Modules:
  0.0 852.9 jit_solution(1161996941468640835)
XLA Ops:
  8.1 20.8 %fusion.43 = f32[1024,128]{1,0:T(8,128)S(1)} fusion(bf16[1024,128]{1,0:T(8,128)(2,1)S(1)} %copy-done), kind=kOutput, calls=%fused_computation.93 | convolution fusion | flops 1626341376 | bytes 786432 | tf_op jit(solution)/shard_map/mc,mk->kc/dot_general | solution.py:112
  30.1 22.3 %all-gather.2.cloned.1.call-done = bf16[4,1024,512]{2,1,0:T(8,128)(2,1)} async-done(((bf16[4,1024,128]{2,1,0:T(8,128)(2,1)}), bf16[4,1024,512]{2,1,0:T(8,128)(2,1)}) %all-gather.2.cloned.1.call-update) | async-done | bytes 4194320 | tf_op jit(solution)/shard_map/all_gather | solution.py:86
  88.5 17.2 %fusion.26 = f32[1024,4,128]{2,0,1:T(8,128)S(1)} fusion(bf16[4,1024,256]{1,2,0:T(8,128)(2,1)S(1)} %add_convert_fusion), kind=kOutput, calls=%fused_computation.67 | convolution fusion | flops 1093664768 | bytes 3145728 | tf_op jit(solution)/shard_map/rwc,wk->rkc/dot_general | solution.py:109
  105.7 18.4 %add_bitcast_fusion = f32[4,1024,128]{2,1,0:T(8,128)S(1)} fusion(f32[1024,4,128]{2,0,1:T(8,128)S(1)} %fusion.26, bf16[4,1024,256]{1,2,0:T(8,128)(2,1)} %copy-done.11), kind=kOutput, calls=%fused_computation.90 | convolution fusion | flops 1091043328 | bytes 5242880 | tf_op jit(solution)/shard_map/rwc,wk->rkc/dot_general | solution.py:108
  125.7 17.4 %rev.25 = f32[4,1023,128]{2,1,0:T(8,128)} reverse(f32[4,1023,128]{2,1,0:T(8,128)} %slice.247), dimensions={1} | reverse | bytes 4190208 | tf_op jit(solution)/shard_map/jit(_flip)/rev | solution.py:51
  145.1 30.1 %multiply_bitcast_fusion.1 = f32[4,1024,128]{1,2,0:T(8,128)S(1)} fusion(f32[4,1024,128]{2,1,0:T(8,128)S(1)} %fusion.175), kind=kOutput, calls=%fused_computation.86 | convolution fusion | flops 6458703872 | bytes 4194304 | tf_op jit(solution)/shard_map/rkc,kw->rwc/dot_general | solution.py:115
  177.1 8.8 %all-to-all-start = ((f32[4,1024,128]{2,0,1:T(4,128)}), f32[4,1024,128]{2,0,1:T(4,128)S(1)}, u32[]{:S(2)}, u32[]{:S(2)}) async-start(f32[4,1024,128]{2,0,1:T(4,128)} %copy.99), calls=%async_computation | async-start | bytes 4194304 | tf_op jit(solution)/shard_map/all_to_all | solution.py:125
  189.2 22.6 %all-to-all-done = f32[4,1024,128]{2,0,1:T(4,128)S(1)} async-done(((f32[4,1024,128]{2,0,1:T(4,128)}), f32[4,1024,128]{2,0,1:T(4,128)S(1)}, u32[]{:S(2)}, u32[]{:S(2)}) %all-to-all-start) | async-done | bytes 2097184 | tf_op jit(solution)/shard_map/all_to_all | solution.py:125
  217.0 16.6 %rev.27 = f32[127,32,128]{2,0,1:T(8,128)} reverse(f32[127,32,128]{2,0,1:T(8,128)} %slice.251), dimensions={0} | reverse | bytes 4161536 | tf_op jit(solution)/shard_map/jit(_flip)/rev | solution.py:51
  250.8 25.1 %all-to-all-done.1 = f32[128,32,128]{2,1,0:T(8,128)S(1)} async-done(((f32[128,32,128]{2,1,0:T(8,128)}), f32[128,32,128]{2,1,0:T(8,128)S(1)}, u32[]{:S(2)}, u32[]{:S(2)}) %all-to-all-start.1) | async-done | bytes 2097184 | tf_op jit(solution)/shard_map/all_to_all | solution.py:127
  285.9 33.2 %all_to_all.77 = f32[4,1024,128]{2,0,1:T(4,128)S(1)} all-to-all(f32[4,1024,128]{2,0,1:T(4,128)S(1)} %copy.107), channel_id=1, replica_groups=mesh['grid'=32,'ch'=4] {'grid'}, dimensions={1} | all-to-all | bytes 4194304 | tf_op jit(solution)/shard_map/all_to_all | solution.py:128
  324.5 16.6 %rev.28 = f32[127,32,128]{2,0,1:T(8,128)} reverse(f32[127,32,128]{2,0,1:T(8,128)} %slice.253), dimensions={0} | reverse | bytes 4161536 | tf_op jit(solution)/shard_map/jit(_flip)/rev | solution.py:51
  353.0 17.9 %fusion.178 = f32[1024,1024,1]{1,0,2:T(8,128)} fusion(), kind=kLoop, calls=%fused_computation.39.clone.clone.clone.1 | loop fusion | flops 15728640 | bytes 4194304 | tf_op jit(solution)/shard_map/rwc,wk->rkc/dot_general | solution.py:135
  370.9 17.5 %sine_add_fusion.20 = f32[1024,1024]{1,0:T(8,128)} fusion(), kind=kLoop, calls=%fused_computation.52.clone.1.clone.1 | loop fusion | flops 15728640 | bytes 4194304
  399.6 17.1 %rev.29 = f32[4,1023,128]{2,1,0:T(8,128)} reverse(f32[4,1023,128]{2,1,0:T(8,128)} %slice.255), dimensions={1} | reverse | bytes 4190208 | tf_op jit(solution)/shard_map/jit(_flip)/rev | solution.py:51
  424.6 9.1 %fusion.41 = f32[1024,512]{0,1:S(1)} fusion(f32[1024,512]{0,1:T(8,128)S(1)} %bitcast.133, f32[1024,1024]{1,0:T(8,128)} %sine_add_fusion.20), kind=kOutput, calls=%fused_computation.91 | convolution fusion | flops 6442450944 | bytes 8388608
  441.3 25.0 %fusion.64 = bf16[1024,128]{1,0:T(8,128)(2,1)} fusion(f32[1024,128]{1,0:T(8,128)S(1)} %copy-done.14), kind=kOutput, calls=%fused_computation.102 | convolution fusion | flops 1626603520 | bytes 786432 | tf_op jit(solution)/shard_map/kc,km->mc/dot_general | solution.py:141
  466.4 8.7 %select_maximum_fusion = f32[6,1026,256]{1,2,0:T(8,128)} fusion(f32[1,1024,256]{1,2,0:T(8,128)} %collective-permute-done.3, f32[1,1024,256]{1,2,0:T(8,128)S(1)} %collective-permute-done.2, f32[4,1024,128]{1,2,0:T(8,128)S(1)} %multiply_bitcast_fusion, f32[4,1024,128]{1,2,0:T(8,128)} %get-tuple-element.56), kind=kLoop, calls=%fused_computation.2 | loop fusion | flops 15759360 | bytes 12595200 | tf_op jit(solution)/shard_map/concatenate | solution.py:19
  475.1 15.5 %fusion.5 = bf16[4,1024,256]{1,2,0:T(8,128)(2,1)} fusion(f32[6,1026,256]{1,2,0:T(8,128)} %select_maximum_fusion, f32[1,1024,256]{1,2,0:T(8,128)S(1)} %collective-permute-done.2, f32[4,1024,128]{1,2,0:T(8,128)S(1)} %multiply_bitcast_fusion, f32[4,1024,128]{1,2,0:T(8,128)} %get-tuple-element.56, f32[1,1024,256]{1,2,0:T(8,128)} %collective-permute-done.3, ...), kind=kLoop, calls=%fused_computation.19 | loop fusion | flops 24117248 | bytes 33563648 | tf_op jit(solution)/shard_map/convert_element_type | solution.py:168
  523.1 19.8 %multiply_reduce_fusion.7 = (f32[256]{0:T(256)S(1)}, f32[256]{0:T(256)S(1)}, f32[256]{0:T(256)S(1)}, f32[256]{0:T(256)S(1)}, f32[256]{0:T(256)S(1)}, /*index=5*/...) fusion(f32[6,1026,256]{1,2,0:T(8,128)} %copy-done.2, f32[4,1024,128]{1,2,0:T(8,128)S(1)} %multiply_bitcast_fusion, ...), kind=kLoop, calls=%fused_computation.49 | loop fusion | flops 19920640 | bytes 41952256 | tf_op jit(solution)/shard_map/reduce_sum | solution.py:161
  543.8 9.0 %all-to-all-start.4 = ((f32[32,2,3,3,128]{4,1,3,2,0:T(2,128)}), f32[32,2,3,3,128]{4,1,3,2,0:T(2,128)S(1)}, u32[]{:S(2)}, u32[]{:S(2)}) async-start(f32[32,2,3,3,128]{4,1,3,2,0:T(2,128)} %broadcast_in_dim.2), calls=%async_computation.4 | async-start | bytes 589824 | tf_op jit(solution)/shard_map/all_to_all | solution.py:25
  553.3 132.1 %all-reduce.2 = bf16[128,128]{1,0:T(8,128)(2,1)S(1)} all-reduce(bf16[128,128]{1,0:T(8,128)(2,1)S(1)} %fusion.67), channel_id=5, replica_groups=mesh['grid'=32,'ch'=4] {'grid'}, use_global_device_ids=true, to_apply=%region_15.16.clone | all-reduce | flops 16384 | bytes 65536
  687.9 79.1 %reduce-scatter.12.cloned.1.call-done = bf16[16,256]{1,0:T(8,128)(2,1)} async-done(((bf16[512,256]{1,0:T(8,128)(2,1)}), bf16[16,256]{1,0:T(8,128)(2,1)}) %reduce-scatter.12.cloned.1.call-update) | async-done | bytes 8208
  769.4 73.2 %reduce-scatter.10.cloned.1.call-done = bf16[128,4096]{1,0:T(8,128)(2,1)} async-done(((bf16[512,4096]{1,0:T(8,128)(2,1)}), bf16[128,4096]{1,0:T(8,128)(2,1)}) %reduce-scatter.10.cloned.1.call-update) | async-done | bytes 1048592
  (135 shorter events, 164.4 us)
Async XLA Ops:
  7.2 45.2 %all-gather.2.cloned.1.call-start = ((), (), s32[]{:S(2)}) async-start(), calls=%async_computation.8 | async-start | bytes 5242880 | tf_op jit(solution)/shard_map/all_gather | solution.py:86
  8.1 21.7 %copy-start.16 = (bf16[512,128]{1,0:T(8,128)(2,1)S(1)}, bf16[512,128]{1,0:T(8,128)(2,1)}, u32[]{:S(2)}) copy-start(bf16[512,128]{1,0:T(8,128)(2,1)} %param.8) | copy-start | bytes 393220
  8.1 21.8 %copy-start.17 = (bf16[512,128]{1,0:T(8,128)(2,1)S(1)}, bf16[512,128]{1,0:T(8,128)(2,1)}, u32[]{:S(2)}) copy-start(bf16[512,128]{1,0:T(8,128)(2,1)} %param.9) | copy-start | bytes 393220
  30.1 32.1 %copy-start.18 = (bf16[2,3,3,128]{3,0,2,1:T(2,128)(2,1)S(1)}, bf16[2,3,3,128]{3,0,2,1:T(2,128)(2,1)}, u32[]{:S(2)}) copy-start(bf16[2,3,3,128]{3,0,2,1:T(2,128)(2,1)} %param.10) | copy-start | bytes 13828
  30.1 34.9 %slice-start = ((f32[1024,128]{1,0:T(8,128)}), f32[1,128]{1,0:T(1,128)S(1)}, s32[]{:S(2)}) async-start(f32[1024,128]{1,0:T(8,128)} %copy-done.13), calls=%async_computation.12 | async-start | bytes 1024 | tf_op jit(solution)/shard_map/slice | solution.py:49
  56.9 14.5 %collective-permute-start = (bf16[1,1024,256]{1,2,0:T(8,128)(2,1)}, bf16[1,1024,256]{1,2,0:T(8,128)(2,1)}, u32[]{:S(2)}, u32[]{:S(2)}) collective-permute-start(bf16[1,1024,256]{1,2,0:T(8,128)(2,1)} %get-tuple-element.57), channel_id=1, source_target_pairs={{0,4},{4,8},{8,12},{12,16},{16,20},{20,24},{24,28},{28,32},{32,36}... | collective-permute-start | bytes 1572872 | tf_op jit(solution)/shard_map/ppermute | solution.py:17
  60.9 15.1 %collective-permute-start.1 = (bf16[1,1024,256]{1,2,0:T(8,128)(2,1)}, bf16[1,1024,256]{1,2,0:T(8,128)(2,1)}, u32[]{:S(2)}, u32[]{:S(2)}) collective-permute-start(bf16[1,1024,256]{1,2,0:T(8,128)(2,1)} %get-tuple-element.58), channel_id=1, source_target_pairs={{4,0},{8,4},{12,8},{16,12},{20,16},{24,20},{28,24},{32,28},{36,32}... | collective-permute-start | bytes 1572872 | tf_op jit(solution)/shard_map/ppermute | solution.py:18
  79.2 7.9 copy-start.2
  124.1 19.1 %copy-start.7 = (f32[4,1024,128]{2,1,0:T(8,128)}, f32[4,1024,128]{2,1,0:T(8,128)S(1)}, u32[]{:S(2)}) copy-start(f32[4,1024,128]{2,1,0:T(8,128)S(1)} %add_bitcast_fusion) | copy-start | bytes 6291460
  175.2 10.7 %copy-start.19 = (bf16[128,128]{1,0:T(8,128)(2,1)S(1)}, bf16[128,128]{1,0:T(8,128)(2,1)}, u32[]{:S(2)}) copy-start(bf16[128,128]{1,0:T(8,128)(2,1)} %param.12) | copy-start | bytes 98308
  177.1 34.6 %all-to-all-start = ((f32[4,1024,128]{2,0,1:T(4,128)}), f32[4,1024,128]{2,0,1:T(4,128)S(1)}, u32[]{:S(2)}, u32[]{:S(2)}) async-start(f32[4,1024,128]{2,0,1:T(4,128)} %copy.99), calls=%async_computation | async-start | bytes 4194304 | tf_op jit(solution)/shard_map/all_to_all | solution.py:125
  215.4 18.2 %copy-start.5 = (f32[128,32,128]{2,0,1:T(8,128)}, f32[128,32,128]{2,0,1:T(8,128)S(1)}, u32[]{:S(2)}) copy-start(f32[128,32,128]{2,0,1:T(8,128)S(1)} %fusion.85) | copy-start | bytes 6291460
  240.2 35.7 %all-to-all-start.1 = ((f32[128,32,128]{2,1,0:T(8,128)}), f32[128,32,128]{2,1,0:T(8,128)S(1)}, u32[]{:S(2)}, u32[]{:S(2)}) async-start(f32[128,32,128]{2,1,0:T(8,128)} %copy.102), calls=%async_computation.1 | async-start | bytes 4194304 | tf_op jit(solution)/shard_map/all_to_all | solution.py:127
  322.8 18.2 %copy-start.6 = (f32[128,32,128]{2,0,1:T(8,128)}, f32[128,32,128]{2,0,1:T(8,128)S(1)}, u32[]{:S(2)}) copy-start(f32[128,32,128]{2,0,1:T(8,128)S(1)} %fusion.82) | copy-start | bytes 6291460
  347.7 40.8 %all-to-all-start.3 = ((f32[128,32,128]{2,1,0:T(8,128)}), f32[128,32,128]{2,1,0:T(8,128)S(1)}, u32[]{:S(2)}, u32[]{:S(2)}) async-start(f32[128,32,128]{2,1,0:T(8,128)} %copy.110), calls=%async_computation.3 | async-start | bytes 4194304 | tf_op jit(solution)/shard_map/all_to_all | solution.py:132
  352.9 333.7 %reduce-scatter.8.cloned.1.call-start = ((), (), s32[]{:S(2)}) async-start(), calls=%async_computation.9 | async-start | bytes 270336 | tf_op jit(solution)/shard_map/reduce_scatter | solution.py:189
  397.4 19.2 %copy-start.8 = (f32[4,1024,128]{2,1,0:T(8,128)S(1)}, f32[4,1024,128]{2,1,0:T(8,128)}, u32[]{:S(2)}) copy-start(f32[4,1024,128]{2,1,0:T(8,128)} %copy-done.7) | copy-start | bytes 6291460
  433.9 7.4 copy-start.14
  436.8 29.6 %collective-permute-start.2 = (f32[1,1024,256]{1,2,0:T(8,128)}, f32[1,1024,256]{1,2,0:T(8,128)S(1)}, u32[]{:S(2)}, u32[]{:S(2)}) collective-permute-start(f32[1,1024,256]{1,2,0:T(8,128)} %get-tuple-element.52), channel_id=1, source_target_pairs={{0,4},{4,8},{8,12},{12,16},{16,20},{20,24},{24,28},{28,32},{32,36}... | collective-permute-start | bytes 3145736 | tf_op jit(solution)/shard_map/ppermute | solution.py:17
  440.0 26.4 %collective-permute-start.3 = (f32[1,1024,256]{1,2,0:T(8,128)}, f32[1,1024,256]{1,2,0:T(8,128)}, u32[]{:S(2)}, u32[]{:S(2)}) collective-permute-start(f32[1,1024,256]{1,2,0:T(8,128)} %get-tuple-element.53), channel_id=1, source_target_pairs={{4,0},{8,4},{12,8},{16,12},{20,16},{24,20},{28,24},{32,28},{36,32}... | collective-permute-start | bytes 3145736 | tf_op jit(solution)/shard_map/ppermute | solution.py:18
  466.3 300.7 %reduce-scatter.12.cloned.1.call-start = ((), (), s32[]{:S(2)}) async-start(), calls=%async_computation.11 | async-start | bytes 270336
  495.6 347.0 %reduce-scatter.10.cloned.1.call-start = ((), (), s32[]{:S(2)}) async-start(), calls=%async_computation.10 | async-start | bytes 5242880
  523.1 323.0 %copy-start.1 = (bf16[1024,128]{1,0:T(8,128)(2,1)S(1)}, bf16[1024,128]{1,0:T(8,128)(2,1)}, u32[]{:S(2)}) copy-start(bf16[1024,128]{1,0:T(8,128)(2,1)} %param.11) | copy-start | bytes 786436
  543.8 142.2 %all-to-all-start.4 = ((f32[32,2,3,3,128]{4,1,3,2,0:T(2,128)}), f32[32,2,3,3,128]{4,1,3,2,0:T(2,128)S(1)}, u32[]{:S(2)}, u32[]{:S(2)}) async-start(f32[32,2,3,3,128]{4,1,3,2,0:T(2,128)} %broadcast_in_dim.2), calls=%async_computation.4 | async-start | bytes 589824 | tf_op jit(solution)/shard_map/all_to_all | solution.py:25
  (10 other events, 16.7 us)
Sparse Core Ops, SparseCore 0:
  9.7 42.6 all-gather.1
  466.4 140.0 reduce-scatter.7
  608.9 158.1 reduce-scatter.11
  769.5 72.9 reduce-scatter.9
where the time goes:
time: 865 us; the launch traced here: 853 us
  waiting for transfers between devices  233 us (27%)
  blocking collectives  165 us (19%)
  matrix products  153 us (18%)
  local copies, waits for them, and re-layouts  130 us (15%)
  other arithmetic  115 us (13%)
  starting transfers between devices  41.3 us (5%)
  between operations  15.3 us (2%)
    unnamed x6, waiting for transfers between devices  153 us
    unnamed x1, blocking collectives  132 us
    rev x6, local copies, waits for them, and re-layouts, mirror(): return jnp.concatenate([leading, jnp.flip(remainder, along)], axis=along)  71.1 us
    all_to_all x1, blocking collectives, local(): lax.all_to_all(grad_mix, 'grid', split_axis=1, concat_axis=0, tiled=True)  33.2 us
    unnamed x58, local copies, waits for them, and re-layouts  32.9 us
    dot_general x1, matrix products, local(): jnp.einsum('rkc,kw->rwc', row_mixed, cas_width, precision=highest)  30.1 us
    all_to_all x1, waiting for transfers between devices, local(): lax.all_to_all(mixed_cols, 'grid', split_axis=0, concat_axis=1, tiled=True)  25.1 us
    dot_general x1, matrix products, local(): jnp.einsum('kc,km->mc', row_term, cas_width, precision=highest)  25 us
  transfers between devices with their start and end apart: 12, of which 7 were waited for; matrix products, arithmetic and copies ran while one was open for 20% of the time, Pallas kernels for 0%

commit v1 on v0

--- a/solution.py
+++ b/solution.py
@@ -83,7 +83,9 @@
 
 def local(inputs, w_gate, w_value, short_filter, row_filter, column_filter, cotangent):
     tile_rows, full_width, channels = inputs.shape
-    gathered = lax.all_gather(inputs, "ch", axis=2, tiled=True)
+    gathered = jnp.concatenate(
+        lax.all_to_all(jnp.stack([inputs] * lax.axis_size("ch")), "ch", 0, 0), axis=2
+    )
     w_both = jnp.concatenate([w_gate, w_value], axis=1)
     stacked = jnp.einsum(
         "rwd,dc->rwc", gathered, w_both, preferred_element_type=jnp.float32

time: 865 us -> 880 us (1.017)
    all_to_all x0 -> x1, waiting for transfers between devices: none -> 26.8 us  [local(): lax.all_to_all(jnp.stack([inputs] * lax.axis_size('ch')), 'ch', 0, 0)]
    all_gather x1 -> x0, waiting for transfers between devices: 22.3 us -> none  [local(): gathered = lax.all_gather(inputs, 'ch', axis=2, tiled=True)]
    unnamed x6 -> x5, waiting for transfers between devices: 153 us -> 152 us
    unnamed x58 -> x100, local copies, waits for them, and re-layouts: 32.9 us -> 32.7 us
where the time goes in v1:
time: 880 us; the launch traced here: 868 us
  waiting for transfers between devices  235 us (27%)
  blocking collectives  168 us (19%)
  matrix products  153 us (17%)
  local copies, waits for them, and re-layouts  135 us (15%)
  other arithmetic  114 us (13%)
  starting transfers between devices  47.8 us (5%)
  between operations  15.5 us (2%)
    unnamed x5, waiting for transfers between devices  152 us
    unnamed x1, blocking collectives  133 us
    rev x6, local copies, waits for them, and re-layouts, mirror(): return jnp.concatenate([leading, jnp.flip(remainder, along)], axis=along)  71.1 us
    all_to_all x1, blocking collectives, local(): lax.all_to_all(grad_mix, 'grid', split_axis=1, concat_axis=0, tiled=True)  34.9 us
    unnamed x100, local copies, waits for them, and re-layouts  32.7 us
    dot_general x1, matrix products, local(): jnp.einsum('rkc,kw->rwc', row_mixed, cas_width, precision=highest)  30.1 us
    all_to_all x1, waiting for transfers between devices, local(): lax.all_to_all(jnp.stack([inputs] * lax.axis_size('ch')), 'ch', 0, 0)  26.8 us
    dot_general x1, matrix products, local(): jnp.einsum('kc,km->mc', row_term, cas_width, precision=highest)  25 us
  transfers between devices with their start and end apart: 12, of which 7 were waited for; matrix products, arithmetic and copies ran while one was open for 20% of the time, Pallas kernels for 0%

profile of v1, /device:TPU:1, one launch (start us, length us, event | category | flops | bytes accessed | tf_op | source)
XLA Modules:
  0.0 867.6 jit_solution(16025284194241572262)
XLA Ops:
  17.5 20.9 %fusion.49 = f32[1024,128]{1,0:T(8,128)S(1)} fusion(bf16[1024,128]{1,0:T(8,128)(2,1)S(1)} %copy-done), kind=kOutput, calls=%fused_computation.99 | convolution fusion | flops 1626341376 | bytes 786432 | tf_op jit(solution)/shard_map/mc,mk->kc/dot_general | solution.py:114
  39.5 26.8 %all-to-all-done = bf16[4,4,1024,128]{3,2,1,0:T(8,128)(2,1)} async-done(((bf16[4,4,1024,128]{3,2,1,0:T(8,128)(2,1)}), bf16[4,4,1024,128]{3,2,1,0:T(8,128)(2,1)}, u32[]{:S(2)}, u32[]{:S(2)}) %all-to-all-start) | async-done | bytes 4194336 | tf_op jit(solution)/shard_map/all_to_all | solution.py:87
  102.3 17.2 %fusion.32 = f32[1024,4,128]{2,0,1:T(8,128)S(1)} fusion(bf16[4,1024,256]{1,2,0:T(8,128)(2,1)S(1)} %add_convert_fusion), kind=kOutput, calls=%fused_computation.73 | convolution fusion | flops 1093664768 | bytes 3145728 | tf_op jit(solution)/shard_map/rwc,wk->rkc/dot_general | solution.py:111
  119.4 18.4 %add_bitcast_fusion = f32[4,1024,128]{2,1,0:T(8,128)S(1)} fusion(f32[1024,4,128]{2,0,1:T(8,128)S(1)} %fusion.32, bf16[4,1024,256]{1,2,0:T(8,128)(2,1)} %copy-done.11), kind=kOutput, calls=%fused_computation.96 | convolution fusion | flops 1091043328 | bytes 5242880 | tf_op jit(solution)/shard_map/rwc,wk->rkc/dot_general | solution.py:110
  139.4 17.4 %rev.25 = f32[4,1023,128]{2,1,0:T(8,128)} reverse(f32[4,1023,128]{2,1,0:T(8,128)} %slice.247), dimensions={1} | reverse | bytes 4190208 | tf_op jit(solution)/shard_map/jit(_flip)/rev | solution.py:51
  158.7 30.1 %multiply_bitcast_fusion.1 = f32[4,1024,128]{1,2,0:T(8,128)S(1)} fusion(f32[4,1024,128]{2,1,0:T(8,128)S(1)} %fusion.192), kind=kOutput, calls=%fused_computation.92 | convolution fusion | flops 6458703872 | bytes 4194304 | tf_op jit(solution)/shard_map/rkc,kw->rwc/dot_general | solution.py:117
  190.7 9.8 %all-to-all-start.1 = ((f32[4,1024,128]{2,0,1:T(4,128)}), f32[4,1024,128]{2,0,1:T(4,128)S(1)}, u32[]{:S(2)}, u32[]{:S(2)}) async-start(f32[4,1024,128]{2,0,1:T(4,128)} %copy.101), calls=%async_computation.1 | async-start | bytes 4194304 | tf_op jit(solution)/shard_map/all_to_all | solution.py:127
  203.1 23.8 %all-to-all-done.1 = f32[4,1024,128]{2,0,1:T(4,128)S(1)} async-done(((f32[4,1024,128]{2,0,1:T(4,128)}), f32[4,1024,128]{2,0,1:T(4,128)S(1)}, u32[]{:S(2)}, u32[]{:S(2)}) %all-to-all-start.1) | async-done | bytes 2097184 | tf_op jit(solution)/shard_map/all_to_all | solution.py:127
  232.2 16.6 %rev.27 = f32[127,32,128]{2,0,1:T(8,128)} reverse(f32[127,32,128]{2,0,1:T(8,128)} %slice.251), dimensions={0} | reverse | bytes 4161536 | tf_op jit(solution)/shard_map/jit(_flip)/rev | solution.py:51
  264.8 23.2 %all-to-all-done.2 = f32[128,32,128]{2,1,0:T(8,128)S(1)} async-done(((f32[128,32,128]{2,1,0:T(8,128)}), f32[128,32,128]{2,1,0:T(8,128)S(1)}, u32[]{:S(2)}, u32[]{:S(2)}) %all-to-all-start.2) | async-done | bytes 2097184 | tf_op jit(solution)/shard_map/all_to_all | solution.py:129
  298.0 34.9 %all_to_all.82 = f32[4,1024,128]{2,0,1:T(4,128)S(1)} all-to-all(f32[4,1024,128]{2,0,1:T(4,128)S(1)} %copy.109), channel_id=1, replica_groups=mesh['grid'=32,'ch'=4] {'grid'}, dimensions={1} | all-to-all | bytes 4194304 | tf_op jit(solution)/shard_map/all_to_all | solution.py:130
  338.8 16.6 %rev.28 = f32[127,32,128]{2,0,1:T(8,128)} reverse(f32[127,32,128]{2,0,1:T(8,128)} %slice.253), dimensions={0} | reverse | bytes 4161536 | tf_op jit(solution)/shard_map/jit(_flip)/rev | solution.py:51
  367.4 17.9 %fusion.195 = f32[1024,1024,1]{1,0,2:T(8,128)} fusion(), kind=kLoop, calls=%fused_computation.43.clone.clone.clone.1 | loop fusion | flops 15728640 | bytes 4194304 | tf_op jit(solution)/shard_map/rwc,wk->rkc/dot_general | solution.py:137
  385.4 17.5 %sine_add_fusion.20 = f32[1024,1024]{1,0:T(8,128)} fusion(), kind=kLoop, calls=%fused_computation.56.clone.1.clone.1 | loop fusion | flops 15728640 | bytes 4194304
  414.0 17.1 %rev.29 = f32[4,1023,128]{2,1,0:T(8,128)} reverse(f32[4,1023,128]{2,1,0:T(8,128)} %slice.255), dimensions={1} | reverse | bytes 4190208 | tf_op jit(solution)/shard_map/jit(_flip)/rev | solution.py:51
  439.0 9.1 %fusion.47 = f32[1024,512]{0,1:S(1)} fusion(f32[1024,512]{0,1:T(8,128)S(1)} %bitcast.154, f32[1024,1024]{1,0:T(8,128)} %sine_add_fusion.20), kind=kOutput, calls=%fused_computation.97 | convolution fusion | flops 6442450944 | bytes 8388608
  455.7 25.0 %fusion.77 = bf16[1024,128]{1,0:T(8,128)(2,1)} fusion(f32[1024,128]{1,0:T(8,128)S(1)} %copy-done.14), kind=kOutput, calls=%fused_computation.108 | convolution fusion | flops 1626603520 | bytes 786432 | tf_op jit(solution)/shard_map/kc,km->mc/dot_general | solution.py:143
  480.9 8.9 %select_maximum_fusion = f32[6,1026,256]{1,2,0:T(8,128)} fusion(f32[1,1024,256]{1,2,0:T(8,128)} %collective-permute-done.3, f32[1,1024,256]{1,2,0:T(8,128)S(1)} %collective-permute-done.2, f32[4,1024,128]{1,2,0:T(8,128)S(1)} %multiply_bitcast_fusion, f32[4,1024,128]{1,2,0:T(8,128)} %get-tuple-element.56), kind=kLoop, calls=%fused_computation.2 | loop fusion | flops 15759360 | bytes 12595200 | tf_op jit(solution)/shard_map/concatenate | solution.py:19
  489.8 15.1 %fusion.9 = bf16[4,1024,256]{1,2,0:T(8,128)(2,1)} fusion(f32[6,1026,256]{1,2,0:T(8,128)} %select_maximum_fusion, f32[1,1024,256]{1,2,0:T(8,128)S(1)} %collective-permute-done.2, f32[4,1024,128]{1,2,0:T(8,128)S(1)} %multiply_bitcast_fusion, f32[4,1024,128]{1,2,0:T(8,128)} %get-tuple-element.56, f32[1,1024,256]{1,2,0:T(8,128)} %collective-permute-done.3, ...), kind=kLoop, calls=%fused_computation.23 | loop fusion | flops 24117248 | bytes 33563648 | tf_op jit(solution)/shard_map/convert_element_type | solution.py:170
  537.3 19.9 %multiply_reduce_fusion.7 = (f32[256]{0:T(256)S(1)}, f32[256]{0:T(256)S(1)}, f32[256]{0:T(256)S(1)}, f32[256]{0:T(256)S(1)}, f32[256]{0:T(256)S(1)}, /*index=5*/...) fusion(f32[6,1026,256]{1,2,0:T(8,128)} %copy-done.2, f32[4,1024,128]{1,2,0:T(8,128)S(1)} %multiply_bitcast_fusion, ...), kind=kLoop, calls=%fused_computation.53 | loop fusion | flops 19920640 | bytes 41952256 | tf_op jit(solution)/shard_map/reduce_sum | solution.py:163
  558.0 9.0 %all-to-all-start.5 = ((f32[32,2,3,3,128]{4,1,3,2,0:T(2,128)}), f32[32,2,3,3,128]{4,1,3,2,0:T(2,128)S(1)}, u32[]{:S(2)}, u32[]{:S(2)}) async-start(f32[32,2,3,3,128]{4,1,3,2,0:T(2,128)} %broadcast_in_dim.2), calls=%async_computation.5 | async-start | bytes 589824 | tf_op jit(solution)/shard_map/all_to_all | solution.py:25
  567.5 132.9 %all-reduce.2 = bf16[128,128]{1,0:T(8,128)(2,1)S(1)} all-reduce(bf16[128,128]{1,0:T(8,128)(2,1)S(1)} %fusion.84), channel_id=5, replica_groups=mesh['grid'=32,'ch'=4] {'grid'}, use_global_device_ids=true, to_apply=%region_15.16.clone | all-reduce | flops 16384 | bytes 65536
  703.0 78.6 %reduce-scatter.12.cloned.1.call-done = bf16[16,256]{1,0:T(8,128)(2,1)} async-done(((bf16[512,256]{1,0:T(8,128)(2,1)}), bf16[16,256]{1,0:T(8,128)(2,1)}) %reduce-scatter.12.cloned.1.call-update) | async-done | bytes 8208
  783.9 73.3 %reduce-scatter.10.cloned.1.call-done = bf16[128,4096]{1,0:T(8,128)(2,1)} async-done(((bf16[512,4096]{1,0:T(8,128)(2,1)}), bf16[128,4096]{1,0:T(8,128)(2,1)}) %reduce-scatter.10.cloned.1.call-update) | async-done | bytes 1048592
  (177 shorter events, 172.2 us)
Async XLA Ops:
  11.3 55.0 %all-to-all-start = ((bf16[4,4,1024,128]{3,2,1,0:T(8,128)(2,1)}), bf16[4,4,1024,128]{3,2,1,0:T(8,128)(2,1)}, u32[]{:S(2)}, u32[]{:S(2)}) async-start(bf16[4,4,1024,128]{3,2,1,0:T(8,128)(2,1)} %stack.49), calls=%async_computation | async-start | bytes 8388608 | tf_op jit(solution)/shard_map/all_to_all | solution.py:87
  17.5 21.7 %copy-start.17 = (bf16[512,128]{1,0:T(8,128)(2,1)S(1)}, bf16[512,128]{1,0:T(8,128)(2,1)}, u32[]{:S(2)}) copy-start(bf16[512,128]{1,0:T(8,128)(2,1)} %param.8) | copy-start | bytes 393220
  17.5 21.8 %copy-start.18 = (bf16[512,128]{1,0:T(8,128)(2,1)S(1)}, bf16[512,128]{1,0:T(8,128)(2,1)}, u32[]{:S(2)}) copy-start(bf16[512,128]{1,0:T(8,128)(2,1)} %param.9) | copy-start | bytes 393220
  39.5 37.1 %copy-start.19 = (bf16[2,3,3,128]{3,0,2,1:T(2,128)(2,1)S(1)}, bf16[2,3,3,128]{3,0,2,1:T(2,128)(2,1)}, u32[]{:S(2)}) copy-start(bf16[2,3,3,128]{3,0,2,1:T(2,128)(2,1)} %param.10) | copy-start | bytes 13828
  39.5 39.9 %slice-start = ((f32[1024,128]{1,0:T(8,128)}), f32[1,128]{1,0:T(1,128)S(1)}, s32[]{:S(2)}) async-start(f32[1024,128]{1,0:T(8,128)} %copy-done.13), calls=%async_computation.12 | async-start | bytes 1024 | tf_op jit(solution)/shard_map/slice | solution.py:49
  70.8 14.2 %collective-permute-start = (bf16[1,1024,256]{1,2,0:T(8,128)(2,1)}, bf16[1,1024,256]{1,2,0:T(8,128)(2,1)}, u32[]{:S(2)}, u32[]{:S(2)}) collective-permute-start(bf16[1,1024,256]{1,2,0:T(8,128)(2,1)} %get-tuple-element.57), channel_id=1, source_target_pairs={{0,4},{4,8},{8,12},{12,16},{16,20},{20,24},{24,28},{28,32},{32,36}... | collective-permute-start | bytes 1572872 | tf_op jit(solution)/shard_map/ppermute | solution.py:17
  75.3 14.4 %collective-permute-start.1 = (bf16[1,1024,256]{1,2,0:T(8,128)(2,1)}, bf16[1,1024,256]{1,2,0:T(8,128)(2,1)}, u32[]{:S(2)}, u32[]{:S(2)}) collective-permute-start(bf16[1,1024,256]{1,2,0:T(8,128)(2,1)} %get-tuple-element.58), channel_id=1, source_target_pairs={{4,0},{8,4},{12,8},{16,12},{20,16},{24,20},{28,24},{32,28},{36,32}... | collective-permute-start | bytes 1572872 | tf_op jit(solution)/shard_map/ppermute | solution.py:18
  79.4 13.6 %copy-start.22 = (f32[1,1,256]{2,1,0:T(1,128)}, f32[1,1,256]{2,1,0:T(1,128)S(1)}, u32[]{:S(2)}) copy-start(f32[1,1,256]{2,1,0:T(1,128)S(1)} %get-tuple-element.65) | copy-start | bytes 3076
  137.8 19.0 %copy-start.7 = (f32[4,1024,128]{2,1,0:T(8,128)}, f32[4,1024,128]{2,1,0:T(8,128)S(1)}, u32[]{:S(2)}) copy-start(f32[4,1024,128]{2,1,0:T(8,128)S(1)} %add_bitcast_fusion) | copy-start | bytes 6291460
  139.4 19.4 %copy-start.20 = (f32[4,1,128]{2,1,0:T(1,128)}, f32[4,1,128]{2,1,0:T(1,128)S(1)}, u32[]{:S(2)}) copy-start(f32[4,1,128]{2,1,0:T(1,128)S(1)} %slice.246) | copy-start | bytes 6148
  190.7 36.2 %all-to-all-start.1 = ((f32[4,1024,128]{2,0,1:T(4,128)}), f32[4,1024,128]{2,0,1:T(4,128)S(1)}, u32[]{:S(2)}, u32[]{:S(2)}) async-start(f32[4,1024,128]{2,0,1:T(4,128)} %copy.101), calls=%async_computation.1 | async-start | bytes 4194304 | tf_op jit(solution)/shard_map/all_to_all | solution.py:127
  230.6 18.3 %copy-start.5 = (f32[128,32,128]{2,0,1:T(8,128)}, f32[128,32,128]{2,0,1:T(8,128)S(1)}, u32[]{:S(2)}) copy-start(f32[128,32,128]{2,0,1:T(8,128)S(1)} %fusion.102) | copy-start | bytes 6291460
  255.4 32.6 %all-to-all-start.2 = ((f32[128,32,128]{2,1,0:T(8,128)}), f32[128,32,128]{2,1,0:T(8,128)S(1)}, u32[]{:S(2)}, u32[]{:S(2)}) async-start(f32[128,32,128]{2,1,0:T(8,128)} %copy.104), calls=%async_computation.2 | async-start | bytes 4194304 | tf_op jit(solution)/shard_map/all_to_all | solution.py:129
  336.6 18.9 %copy-start.6 = (f32[128,32,128]{2,0,1:T(8,128)}, f32[128,32,128]{2,0,1:T(8,128)S(1)}, u32[]{:S(2)}) copy-start(f32[128,32,128]{2,0,1:T(8,128)S(1)} %fusion.99) | copy-start | bytes 6291460
  362.0 40.9 %all-to-all-start.4 = ((f32[128,32,128]{2,1,0:T(8,128)}), f32[128,32,128]{2,1,0:T(8,128)S(1)}, u32[]{:S(2)}, u32[]{:S(2)}) async-start(f32[128,32,128]{2,1,0:T(8,128)} %copy.112), calls=%async_computation.4 | async-start | bytes 4194304 | tf_op jit(solution)/shard_map/all_to_all | solution.py:134
  367.4 334.3 %reduce-scatter.8.cloned.1.call-start = ((), (), s32[]{:S(2)}) async-start(), calls=%async_computation.9 | async-start | bytes 270336 | tf_op jit(solution)/shard_map/reduce_scatter | solution.py:191
  411.9 19.2 %copy-start.8 = (f32[4,1024,128]{2,1,0:T(8,128)S(1)}, f32[4,1024,128]{2,1,0:T(8,128)}, u32[]{:S(2)}) copy-start(f32[4,1024,128]{2,1,0:T(8,128)} %copy-done.7) | copy-start | bytes 6291460
  411.9 19.2 %copy-start.21 = (f32[4,1,128]{2,1,0:T(1,128)S(1)}, f32[4,1,128]{2,1,0:T(1,128)}, u32[]{:S(2)}) copy-start(f32[4,1,128]{2,1,0:T(1,128)} %copy-done.20) | copy-start | bytes 6148
  451.2 29.7 %collective-permute-start.2 = (f32[1,1024,256]{1,2,0:T(8,128)}, f32[1,1024,256]{1,2,0:T(8,128)S(1)}, u32[]{:S(2)}, u32[]{:S(2)}) collective-permute-start(f32[1,1024,256]{1,2,0:T(8,128)} %get-tuple-element.52), channel_id=1, source_target_pairs={{0,4},{4,8},{8,12},{12,16},{16,20},{20,24},{24,28},{28,32},{32,36}... | collective-permute-start | bytes 3145736 | tf_op jit(solution)/shard_map/ppermute | solution.py:17
  454.4 26.5 %collective-permute-start.3 = (f32[1,1024,256]{1,2,0:T(8,128)}, f32[1,1024,256]{1,2,0:T(8,128)}, u32[]{:S(2)}, u32[]{:S(2)}) collective-permute-start(f32[1,1024,256]{1,2,0:T(8,128)} %get-tuple-element.53), channel_id=1, source_target_pairs={{4,0},{8,4},{12,8},{16,12},{20,16},{24,20},{28,24},{32,28},{36,32}... | collective-permute-start | bytes 3145736 | tf_op jit(solution)/shard_map/ppermute | solution.py:18
  480.8 300.8 %reduce-scatter.12.cloned.1.call-start = ((), (), s32[]{:S(2)}) async-start(), calls=%async_computation.11 | async-start | bytes 270336
  509.8 347.4 %reduce-scatter.10.cloned.1.call-start = ((), (), s32[]{:S(2)}) async-start(), calls=%async_computation.10 | async-start | bytes 5242880
  537.3 323.4 %copy-start.1 = (bf16[1024,128]{1,0:T(8,128)(2,1)S(1)}, bf16[1024,128]{1,0:T(8,128)(2,1)}, u32[]{:S(2)}) copy-start(bf16[1024,128]{1,0:T(8,128)(2,1)} %param.11) | copy-start | bytes 786436
  558.0 143.0 %all-to-all-start.5 = ((f32[32,2,3,3,128]{4,1,3,2,0:T(2,128)}), f32[32,2,3,3,128]{4,1,3,2,0:T(2,128)S(1)}, u32[]{:S(2)}, u32[]{:S(2)}) async-start(f32[32,2,3,3,128]{4,1,3,2,0:T(2,128)} %broadcast_in_dim.2), calls=%async_computation.5 | async-start | bytes 589824 | tf_op jit(solution)/shard_map/all_to_all | solution.py:25
  (31 other events, 246.2 us)
Sparse Core Ops, SparseCore 0:
  480.8 140.2 reduce-scatter.7
  623.5 158.0 reduce-scatter.11
  784.3 72.8 reduce-scatter.9
